TPU v7x, 32 devices: a whole 2x2x4 slice. The times are simulated.
32 devices in a mesh: band: 4 (over y, x), patch: 8 (over z, core).
Axes of the slice: x: 2, y: 2, z: 4, core: 2. Of those that a mesh axis runs over, the one named last changes fastest.
Arguments:
- emissivity: float32 [32, 65536], P('band', 'patch'), may hold values from 0.1 to 0.9
- blackbody: float32 [32, 65536], P('band', 'patch'), may hold values from 0.2 to 2
- loss_weights: float32 [32, 65536], P('band', 'patch'), may hold values from 0.5 to 1.5
- view_blocks: bfloat16 [8, 4, 8, 16, 256, 256], P('patch', 'band'), may hold values from 0 to 0.012207031
- column_blocks: int32 [8, 4, 8, 16], P('patch', 'band'), may hold values from 0 to 255, as said below
- patch_owner: int32 [8, 4, 2048, 1], P('patch', 'band'), may hold values from 0 to 31; in each aligned block of 2048 rows (0 to 2047, 2048 to 4095, ..., all dimensions but the last counted through in order) at most 192 rows name the same one
- patch_surface: int32 [8, 4, 2048], P('patch', 'band'), may hold values from 0 to 1023
Outputs:
- radiosity: float32 [32, 8, 4, 2048], P(None, 'patch', 'band')
- surface_grad: float32 [32, 32768], P(None, ('band', 'patch'))
Inputs may be any that keep to these rules, and one draw needn't show every extreme that they name: column_blocks[g, s, r] lists 16 different row-block indices, all among the 96 row blocks of patch groups g - 1, g and g + 1, wrapping around the 8 groups. `patch_owner`: among the 2048 patches of one row-block range no owner is named more than 192 times.
All inputs are finite; a program needn't handle non-finite values.
Results may differ from a plain program's by a relative error of at most 0.0005.
Values may be sent and summed in bfloat16 or wider, within the bound.
No kernel may reach another device: no remote copies, remote signals or barrier semaphores. Data moves between devices by JAX's collectives and lax.ppermute only.
A program may use at most 128 MiB of HBM per device.

v0:
```python
import jax
import jax.numpy as jnp
from jax import lax
from jax.sharding import PartitionSpec as P


def passed_along(block, axis, distance):
    devices = range(lax.axis_size(axis))
    route = [((i - distance) % len(devices), i) for i in devices]
    return lax.ppermute(block, axis, route)


def body(
    emissivity, blackbody, loss_weights, view_blocks, column_blocks, patch_owner, patch_surface
):
    emissive, planck, weighting = (
        lax.all_to_all(emissivity, "band", split_axis=1, concat_axis=0, tiled=True),
        lax.all_to_all(blackbody, "band", split_axis=1, concat_axis=0, tiled=True),
        lax.all_to_all(loss_weights, "band", split_axis=1, concat_axis=0, tiled=True),
    )
    band_count = emissive.shape[0]
    patch_rows = emissive.shape[1]
    rb_count = view_blocks.shape[2]
    depth = view_blocks.shape[3]
    width = view_blocks.shape[4]
    split_count = lax.axis_size("band")
    group_count = lax.axis_size("patch")
    per_group = split_count * rb_count
    block_total = group_count * per_group
    window_start = (lax.axis_index("patch") - 1) * per_group
    offsets = jnp.mod(column_blocks.reshape(rb_count, depth) - window_start, block_total)
    flat_offsets = offsets.reshape(rb_count * depth)
    matrix = view_blocks.reshape(rb_count, depth, width, width)
    emission = emissive * planck
    reflect = 1.0 - emissive

    def window(vector):
        gathered = lax.all_gather(vector, "band", axis=1, tiled=True)
        lower_rows = passed_along(gathered, "patch", 1)
        upper_rows = passed_along(gathered, "patch", -1)
        joined = jnp.concatenate([lower_rows, gathered, upper_rows], axis=1)
        return joined.reshape(band_count, 3 * per_group, width)

    def forward(vector):
        blocks = window(vector)
        picked = blocks[:, offsets]
        result = jnp.einsum("rkij,brkj->bri", matrix, picked, preferred_element_type=jnp.float32)
        return result.reshape(band_count, patch_rows)

    def adjoint(vector):
        partial_terms = jnp.einsum(
            "rkij,bri->brkj",
            matrix,
            vector.reshape(band_count, rb_count, width),
            preferred_element_type=jnp.float32,
        )
        empty = jnp.zeros((band_count, 3 * per_group, width), jnp.float32)
        totals = empty.at[:, flat_offsets].add(
            partial_terms.reshape(band_count, rb_count * depth, width)
        )
        totals = totals.reshape(band_count, 3, split_count, patch_rows)
        from_upper = passed_along(totals[:, 0].astype(jnp.bfloat16), "patch", -1).astype(
            jnp.float32
        )
        from_lower = passed_along(totals[:, 2], "patch", 1)
        combined = totals[:, 1] + from_upper + from_lower
        return lax.psum_scatter(combined, "band", scatter_dimension=1, tiled=True).reshape(
            band_count, patch_rows
        )

    incident_zero = forward(emission.astype(jnp.bfloat16))
    rad_one = emission + reflect * incident_zero
    incident_one = forward(rad_one.astype(jnp.bfloat16))
    radiosity = emission + reflect * incident_one
    adjoint_one = adjoint((reflect * weighting).astype(jnp.bfloat16))
    adjoint_zero = adjoint((reflect * adjoint_one).astype(jnp.bfloat16))
    gradient = (weighting + adjoint_one + adjoint_zero) * planck - (
        weighting * incident_one + adjoint_one * incident_zero
    )
    device_count = split_count * group_count
    capacity = max(2, 3 * patch_rows // device_count)
    surface_count = patch_rows // 2
    owners = patch_owner.reshape(patch_rows)
    locals_index = patch_surface.reshape(patch_rows)
    owner_hits = (owners[:, None] == jnp.arange(device_count, dtype=jnp.int32)[None, :]).astype(
        jnp.int32
    )
    running = jnp.cumsum(owner_hits, axis=0)
    slot_index = jnp.sum(running * owner_hits, axis=1) - 1
    send_values = (
        jnp.zeros((band_count, device_count, capacity), jnp.float32)
        .at[:, owners, slot_index]
        .set(gradient)
    )
    send_labels = (
        jnp.full((1, device_count, capacity), surface_count, jnp.int32)
        .at[0, owners, slot_index]
        .set(locals_index)
    )
    got_values, got_labels = (
        lax.all_to_all(send_values, ("band", "patch"), split_axis=1, concat_axis=1, tiled=True),
        lax.all_to_all(send_labels, ("band", "patch"), split_axis=1, concat_axis=1, tiled=True),
    )
    flat_values = got_values.reshape(band_count, device_count * capacity)
    flat_labels = got_labels.reshape(device_count * capacity)
    surface_sums = jax.ops.segment_sum(flat_values.T, flat_labels, surface_count + 1)[
        :surface_count
    ].T
    surface_counts = jax.ops.segment_sum(
        jnp.ones((device_count * capacity,), jnp.float32), flat_labels, surface_count + 1
    )[:surface_count]
    surface_grad = surface_sums / jnp.maximum(surface_counts, 1.0)[None, :]
    return (radiosity.reshape(band_count, 1, 1, patch_rows), surface_grad)


def solution(mesh):
    in_specs = (
        P("band", "patch"),
        P("band", "patch"),
        P("band", "patch"),
        P("patch", "band", None, None, None, None),
        P("patch", "band", None, None),
        P("patch", "band", None, None),
        P("patch", "band", None),
    )
    out_specs = (P(None, "patch", "band", None), P(None, ("band", "patch")))
    return jax.shard_map(body, mesh=mesh, in_specs=in_specs, out_specs=out_specs, check_vma=False)
```

profile of v0, /device:TPU:1, one launch (start us, length us, event | category | flops | bytes accessed | tf_op | source)
XLA Modules:
  0.0 336.8 jit_solution(3225798159353689433)
XLA Ops:
  7.2 4.3 %all-to-all-start = ((f32[8,4,2048]{2,0,1:T(8,128)}), f32[8,4,2048]{2,0,1:T(8,128)S(1)}, u32[]{:S(2)}, u32[]{:S(2)}) async-start(f32[8,4,2048]{2,0,1:T(8,128)} %bitcast.215), calls=%async_computation | async-start | bytes 524288 | tf_op jit(solution)/shard_map/all_to_all | solution.py:17
  12.3 0.7 fusion.35
  13.1 9.1 %reduce-window.6 = s32[32,16,128]{2,1,0:T(8,128)S(1)} reduce-window(s32[32,16,128]{2,1,0:T(8,128)S(1)} %fusion.35, s32[]{:T(128)} %constant.21.clone.1), window={size=1x1x128 pad=0_0x0_0x127_0}, to_apply=%region_0.1 | reduce-window | flops 8323072 | bytes 524292 | tf_op jit(solution)/shard_map/reduce-window
  22.9 0.8 fusion.23
  23.7 0.7 compare_select_fusion
  24.4 0.7 multiply_reduce_fusion.1
  25.1 0.8 and_reduce_fusion
  26.1 8.2 %scatter_custom_fusion.4 = s32[6144]{0:T(1024)S(1)} fusion(s32[2048]{0:T(1024)S(1)} %broadcast_select_fusion.1, s32[2048]{0:T(1024)} %bitcast.222, s32[]{:T(128)} %constant.29.clone.1), kind=kCustom, calls=%fused_computation.78 | custom fusion | bytes 25088
  34.4 0.7 reshape.309
  35.1 3.6 %all-to-all-start.3 = ((f32[8,4,2048]{2,0,1:T(8,128)}), f32[8,4,2048]{2,0,1:T(8,128)S(1)}, u32[]{:S(2)}, u32[]{:S(2)}) async-start(f32[8,4,2048]{2,0,1:T(8,128)} %bitcast.30), calls=%async_computation.3 | async-start | bytes 524288 | tf_op jit(solution)/shard_map/all_to_all | solution.py:19
  38.9 4.1 %all-to-all-done.3 = f32[8,4,2048]{2,0,1:T(8,128)S(1)} async-done(((f32[8,4,2048]{2,0,1:T(8,128)}), f32[8,4,2048]{2,0,1:T(8,128)S(1)}, u32[]{:S(2)}, u32[]{:S(2)}) %all-to-all-start.3) | async-done | bytes 262176 | tf_op jit(solution)/shard_map/all_to_all | solution.py:19
  43.0 4.1 %all-to-all-start.1 = ((f32[8,4,2048]{2,0,1:T(8,128)}), f32[8,4,2048]{2,0,1:T(8,128)}, u32[]{:S(2)}, u32[]{:S(2)}) async-start(f32[8,4,2048]{2,0,1:T(8,128)} %bitcast.2), calls=%async_computation.1 | async-start | bytes 524288 | tf_op jit(solution)/shard_map/all_to_all | solution.py:18
  47.2 10.6 %fusion.2 = f32[8,32,16,256]{3,1,2,0:T(8,128)} fusion(bf16[1,1,8,16,256,256]{5,4,3,2,1,0:T(8,128)(2,1)} %param.10, bf16[32,8,256,1]{2,1,0,3:T(8,128)(2,1)S(1)} %bitcast.214), kind=kOutput, calls=%fused_computation.10 | convolution fusion | flops 536870912 | bytes 21102592 | tf_op jit(solution)/shard_map/rkij,bri->brkj/dot_general | solution.py:51
  58.2 13.5 %scatter_fusion = f32[32,96,256]{2,0,1:T(8,128)S(1)} fusion(f32[32,96,256]{2,0,1:T(8,128)S(1)} %broadcast.223.clone, s32[128]{0:T(128)S(1)} %fusion.45, f32[128,32,256]{2,1,0:T(8,128)} %bitcast.195), kind=kCustom, calls=%fused_computation.2 | custom fusion | flops 1048576 | bytes 12583424 | tf_op jit(solution)/shard_map/scatter-add | solution.py:58
  71.7 3.5 %copy.102 = f32[32,96,256]{2,1,0:T(8,128)} copy(f32[32,96,256]{2,0,1:T(8,128)S(1)} %scatter_fusion) | data formatting | bytes 6291456 | tf_op jit(solution)/shard_map/scatter-add | solution.py:58
  75.1 3.4 %reshape.298 = f32[32,3,4,2048]{3,2,1,0:T(4,128)S(1)} reshape(f32[32,96,256]{2,1,0:T(8,128)} %copy.102) | data formatting | bytes 6291456 | tf_op jit(solution)/shard_map/reshape | solution.py:61
  78.6 1.5 fusion.47
  80.1 3.8 %collective-permute-start.5 = (f32[32,4,2048]{2,1,0:T(4,128)}, f32[32,4,2048]{2,1,0:T(4,128)}, u32[]{:S(2)}, u32[]{:S(2)}) collective-permute-start(f32[32,4,2048]{2,1,0:T(4,128)} %get-tuple-element.19), channel_id=1, source_target_pairs={{7,0},{0,1},{1,2},{2,3},{3,4},{4,5},{5,6},{6,7},{15,8},{8,9},{9,10... | collective-permute-start | bytes 3145736 | tf_op jit(solution)/shard_map/ppermute | solution.py:10
  83.9 1.0 fusion.17
  84.9 6.6 %all-to-all-start.2 = ((s32[1,32,192]{2,0,1:T(1,128)}), s32[1,32,192]{2,0,1:T(1,128)S(1)}, u32[]{:S(2)}, u32[]{:S(2)}) async-start(s32[1,32,192]{2,0,1:T(1,128)} %reshape.309), calls=%async_computation.2 | async-start | bytes 65536 | tf_op jit(solution)/shard_map/all_to_all | solution.py:102
  91.6 1.0 fusion.38
  92.5 9.1 %all_gather.6 = bf16[32,8192]{1,0:T(8,128)(2,1)S(1)} all-gather(bf16[32,2048]{1,0:T(8,128)(2,1)S(1)} %fusion.38), channel_id=1, replica_groups=mesh['band'=4,'patch'=8] {'band'}, dimensions={1}, use_global_device_ids=true | all-gather | bytes 655360 | tf_op jit(solution)/shard_map/all_gather | solution.py:38
  101.6 2.8 collective-permute-start
  104.4 2.0 fusion.16
  106.4 1.6 copy.105
  108.2 5.3 %collective-permute-done = bf16[32,8192]{1,0:T(8,128)(2,1)S(1)} collective-permute-done((bf16[32,8192]{1,0:T(8,128)(2,1)S(1)}, bf16[32,8192]{1,0:T(8,128)(2,1)S(1)}, u32[]{:S(2)}, u32[]{:S(2)}) %collective-permute-start) | collective-permute-done | bytes 524320 | tf_op jit(solution)/shard_map/ppermute | solution.py:10
  113.5 5.5 %collective-permute-done.1 = bf16[32,8192]{1,0:T(8,128)(2,1)S(1)} collective-permute-done((bf16[32,8192]{1,0:T(8,128)(2,1)S(1)}, bf16[32,8192]{1,0:T(8,128)(2,1)S(1)}, u32[]{:S(2)}, u32[]{:S(2)}) %collective-permute-start.1) | collective-permute-done | bytes 524320 | tf_op jit(solution)/shard_map/ppermute | solution.py:10
  119.1 1.4 copy.163
  120.4 2.1 gather_fusion
  122.6 10.8 %fusion.10 = f32[8,4,8,256]{3,2,1,0:T(8,128)S(1)} fusion(bf16[32,8,16,256]{3,0,2,1:T(8,128)(2,1)S(1)} %bitcast.198, bf16[1,1,8,16,256,256]{5,4,3,2,1,0:T(8,128)(2,1)} %param.10), kind=kOutput, calls=%fused_computation.22 | convolution fusion | flops 536870912 | bytes 19136512 | tf_op jit(solution)/shard_map/rkij,brkj->bri/dot_general | solution.py:47
  133.4 0.7 copy.133
  134.1 1.7 reduce-scatter.7.cloned.1.call-done
  135.9 1.0 copy.137
  137.0 10.6 %fusion = f32[8,32,16,256]{3,1,2,0:T(8,128)} fusion(bf16[1,1,8,16,256,256]{5,4,3,2,1,0:T(8,128)(2,1)} %param.10, bf16[32,8,256,1]{2,1,0,3:T(8,128)(2,1)S(1)} %bitcast.213), kind=kOutput, calls=%fused_computation.8 | convolution fusion | flops 536870912 | bytes 21102592 | tf_op jit(solution)/shard_map/rkij,bri->brkj/dot_general | solution.py:51
  147.9 13.5 %scatter_fusion.1 = f32[32,96,256]{2,0,1:T(8,128)S(1)} fusion(f32[32,96,256]{2,0,1:T(8,128)S(1)} %broadcast.223, s32[128]{0:T(128)S(1)} %fusion.45, f32[128,32,256]{2,1,0:T(8,128)} %bitcast.194), kind=kCustom, calls=%fused_computation.3 | custom fusion | flops 1048576 | bytes 12583424 | tf_op jit(solution)/shard_map/scatter-add | solution.py:58
  161.4 3.5 %copy.107 = f32[32,96,256]{2,1,0:T(8,128)} copy(f32[32,96,256]{2,0,1:T(8,128)S(1)} %scatter_fusion.1) | data formatting | bytes 6291456 | tf_op jit(solution)/shard_map/scatter-add | solution.py:58
  164.9 3.4 %reshape.302 = f32[32,3,4,2048]{3,2,1,0:T(4,128)S(1)} reshape(f32[32,96,256]{2,1,0:T(8,128)} %copy.107) | data formatting | bytes 6291456 | tf_op jit(solution)/shard_map/reshape | solution.py:61
  168.5 1.8 collective-permute-start.7
  170.6 1.0 fusion.33
  171.6 9.0 %all_gather.7 = bf16[32,8192]{1,0:T(8,128)(2,1)S(1)} all-gather(bf16[32,2048]{1,0:T(8,128)(2,1)S(1)} %fusion.33), channel_id=1, replica_groups=mesh['band'=4,'patch'=8] {'band'}, dimensions={1}, use_global_device_ids=true | all-gather | bytes 655360 | tf_op jit(solution)/shard_map/all_gather | solution.py:38
  180.7 2.6 collective-permute-start.2
  183.3 1.6 collective-permute-start.3
  184.9 2.1 collective-permute-done.6
  188.1 1.6 copy.110
  189.7 7.9 %collective-permute-done.2 = bf16[32,8192]{1,0:T(8,128)(2,1)S(1)} collective-permute-done((bf16[32,8192]{1,0:T(8,128)(2,1)S(1)}, bf16[32,8192]{1,0:T(8,128)(2,1)S(1)}, u32[]{:S(2)}, u32[]{:S(2)}) %collective-permute-start.2) | collective-permute-done | bytes 524320 | tf_op jit(solution)/shard_map/ppermute | solution.py:10
  197.6 2.6 collective-permute-done.3
  200.4 1.4 copy.162
  201.7 2.1 gather_fusion.1
  203.9 11.0 %fusion.4 = f32[8,32,256,1]{2,1,3,0:T(8,128)S(1)} fusion(bf16[32,8,16,256]{3,0,2,1:T(8,128)(2,1)S(1)} %bitcast.197, bf16[1,1,8,16,256,256]{5,4,3,2,1,0:T(8,128)(2,1)} %param.10), kind=kOutput, calls=%fused_computation.12 | convolution fusion | flops 536870912 | bytes 19136512 | tf_op jit(solution)/shard_map/rkij,brkj->bri/dot_general | solution.py:47
  214.9 5.2 %reduce-scatter.9.cloned.1.call-done = f32[32,1,2048]{2,0,1:T(8,128)} async-done(((f32[32,4,2048]{2,0,1:T(8,128)}), f32[32,1,2048]{2,0,1:T(8,128)}) %reduce-scatter.9.cloned.1.call-update) | async-done | bytes 262160
  220.1 1.2 fusion.29
  221.3 1.3 copy.112
  222.7 6.7 %scatter_custom_fusion.5 = f32[32,6144]{0,1:T(8,128)S(1)} fusion(s32[2048]{0:T(1024)S(1)} %broadcast_select_fusion, f32[2048,32]{1,0:T(8,128)} %copy.112, f32[]{:T(128)} %constant.25.clone.1), kind=kCustom, calls=%fused_computation.20 | custom fusion | bytes 786944
  229.4 2.2 copy.113
  231.6 5.1 %all-to-all-start.4 = ((f32[32,32,192]{2,0,1:T(8,128)}), f32[32,32,192]{2,0,1:T(8,128)S(1)}, u32[]{:S(2)}, u32[]{:S(2)}) async-start(f32[32,32,192]{2,0,1:T(8,128)} %copy.113), calls=%async_computation.4 | async-start | bytes 2097152 | tf_op jit(solution)/shard_map/all_to_all | solution.py:101
  236.9 42.6 %scatter_custom_fusion.3 = f32[1025]{0:T(1024)S(1)} fusion(s32[6144]{0:T(1024)S(1)} %reshape.348, f32[6144]{0:T(1024)S(1)} %broadcast.242, f32[]{:T(128)} %constant.25.clone.1), kind=kCustom, calls=%fused_computation.87 | custom fusion | flops 6144 | bytes 4104 | tf_op jit(solution)/shard_map/scatter-add | solution.py:109
  279.5 1.1 copy.98
  280.7 1.0 fusion.34
  281.7 1.0 copy.116
  283.3 1.3 reshape.305
  284.5 2.0 copy.115
  286.5 41.4 %scatter_custom_fusion.2 = f32[1025,32]{1,0:T(8,128)} fusion(s32[6144]{0:T(1024)S(1)} %reshape.348, f32[6144,32]{1,0:T(8,128)S(1)} %copy.115, f32[]{:T(128)} %constant.25.clone.1), kind=kCustom, calls=%fused_computation.37 | custom fusion | flops 196608 | bytes 131204 | tf_op jit(solution)/shard_map/scatter-add | solution.py:106
  327.9 1.2 fusion.19
  329.2 0.8 copy.117
  (66 shorter events, 5.8 us)
Async XLA Ops:
  7.2 18.8 %copy-start.7 = (s32[3]{0:T(128)S(1)}, s32[3]{0:T(128)}, u32[]{:S(2)}) copy-start(s32[3]{0:T(128)} %constant.59) | copy-start | bytes 40
  7.2 18.9 %copy-start.8 = (s32[3]{0:T(128)S(1)}, s32[3]{0:T(128)}, u32[]{:S(2)}) copy-start(s32[3]{0:T(128)} %constant.62) | copy-start | bytes 40
  7.2 27.9 %all-to-all-start = ((f32[8,4,2048]{2,0,1:T(8,128)}), f32[8,4,2048]{2,0,1:T(8,128)S(1)}, u32[]{:S(2)}, u32[]{:S(2)}) async-start(f32[8,4,2048]{2,0,1:T(8,128)} %bitcast.215), calls=%async_computation | async-start | bytes 524288 | tf_op jit(solution)/shard_map/all_to_all | solution.py:17
  35.1 7.9 %all-to-all-start.3 = ((f32[8,4,2048]{2,0,1:T(8,128)}), f32[8,4,2048]{2,0,1:T(8,128)S(1)}, u32[]{:S(2)}, u32[]{:S(2)}) async-start(f32[8,4,2048]{2,0,1:T(8,128)} %bitcast.30), calls=%async_computation.3 | async-start | bytes 524288 | tf_op jit(solution)/shard_map/all_to_all | solution.py:19
  38.9 18.9 %copy-start.5 = (f32[4,8,8,256]{3,2,1,0:T(8,128)}, f32[4,8,8,256]{3,2,1,0:T(8,128)S(1)}, u32[]{:S(2)}) copy-start(f32[4,8,8,256]{3,2,1,0:T(8,128)S(1)} %copy.135) | copy-start | bytes 786436
  43.0 14.8 %copy-start.3 = (f32[8,4,2048]{2,0,1:T(8,128)}, f32[8,4,2048]{2,0,1:T(8,128)S(1)}, u32[]{:S(2)}) copy-start(f32[8,4,2048]{2,0,1:T(8,128)S(1)} %all-to-all-done.3) | copy-start | bytes 786436
  43.0 41.9 %all-to-all-start.1 = ((f32[8,4,2048]{2,0,1:T(8,128)}), f32[8,4,2048]{2,0,1:T(8,128)}, u32[]{:S(2)}, u32[]{:S(2)}) async-start(f32[8,4,2048]{2,0,1:T(8,128)} %bitcast.2), calls=%async_computation.1 | async-start | bytes 524288 | tf_op jit(solution)/shard_map/all_to_all | solution.py:18
  80.1 24.3 %collective-permute-start.5 = (f32[32,4,2048]{2,1,0:T(4,128)}, f32[32,4,2048]{2,1,0:T(4,128)}, u32[]{:S(2)}, u32[]{:S(2)}) collective-permute-start(f32[32,4,2048]{2,1,0:T(4,128)} %get-tuple-element.19), channel_id=1, source_target_pairs={{7,0},{0,1},{1,2},{2,3},{3,4},{4,5},{5,6},{6,7},{15,8},{8,9},{9,10... | collective-permute-start | bytes 3145736 | tf_op jit(solution)/shard_map/ppermute | solution.py:10
  84.9 19.5 %collective-permute-start.4 = (bf16[32,4,2048]{2,1,0:T(4,128)(2,1)}, bf16[32,4,2048]{2,1,0:T(4,128)(2,1)S(1)}, u32[]{:S(2)}, u32[]{:S(2)}) collective-permute-start(bf16[32,4,2048]{2,1,0:T(4,128)(2,1)} %fusion.17), channel_id=1, source_target_pairs={{1,0},{2,1},{3,2},{4,3},{5,4},{6,5},{7,6},{0,7},{9,8},{10,9},{11,1... | collective-permute-start | bytes 1572872 | tf_op jit(solution)/shard_map/ppermute | solution.py:10
  84.9 146.7 %all-to-all-start.2 = ((s32[1,32,192]{2,0,1:T(1,128)}), s32[1,32,192]{2,0,1:T(1,128)S(1)}, u32[]{:S(2)}, u32[]{:S(2)}) async-start(s32[1,32,192]{2,0,1:T(1,128)} %reshape.309), calls=%async_computation.2 | async-start | bytes 65536 | tf_op jit(solution)/shard_map/all_to_all | solution.py:102
  91.5 44.4 %reduce-scatter.7.cloned.1.call-start = ((), (), s32[]{:S(2)}) async-start(), calls=%async_computation.7 | async-start | bytes 1310720
  101.6 11.9 %collective-permute-start = (bf16[32,8192]{1,0:T(8,128)(2,1)S(1)}, bf16[32,8192]{1,0:T(8,128)(2,1)S(1)}, u32[]{:S(2)}, u32[]{:S(2)}) collective-permute-start(bf16[32,8192]{1,0:T(8,128)(2,1)S(1)} %all_gather.6), channel_id=1, source_target_pairs={{7,0},{0,1},{1,2},{2,3},{3,4},{4,5},{5,6},{6,7},{15,8},{8,9},{9,10... | collective-permute-start | bytes 1572872 | tf_op jit(solution)/shard_map/ppermute | solution.py:10
  104.4 14.6 %collective-permute-start.1 = (bf16[32,8192]{1,0:T(8,128)(2,1)S(1)}, bf16[32,8192]{1,0:T(8,128)(2,1)S(1)}, u32[]{:S(2)}, u32[]{:S(2)}) collective-permute-start(bf16[32,8192]{1,0:T(8,128)(2,1)S(1)} %all_gather.6), channel_id=1, source_target_pairs={{1,0},{2,1},{3,2},{4,3},{5,4},{6,5},{7,6},{0,7},{9,8},{10,9},{11,1... | collective-permute-start | bytes 1572872 | tf_op jit(solution)/shard_map/ppermute | solution.py:10
  108.0 112.1 %reduce-scatter.9.cloned.1.call-start = ((), (), s32[]{:S(2)}) async-start(), calls=%async_computation.8 | async-start | bytes 1310720
  122.6 14.4 %copy-start.6 = (f32[4,8,8,256]{3,2,1,0:T(8,128)S(1)}, f32[4,8,8,256]{3,2,1,0:T(8,128)}, u32[]{:S(2)}) copy-start(f32[4,8,8,256]{3,2,1,0:T(8,128)} %copy-done.5) | copy-start | bytes 786436
  168.3 2.3 copy-start.1
  168.5 19.2 %collective-permute-start.7 = (f32[32,4,2048]{2,1,0:T(4,128)S(1)}, f32[32,4,2048]{2,1,0:T(4,128)S(1)}, u32[]{:S(2)}, u32[]{:S(2)}) collective-permute-start(f32[32,4,2048]{2,1,0:T(4,128)S(1)} %get-tuple-element.17), channel_id=1, source_target_pairs={{7,0},{0,1},{1,2},{2,3},{3,4},{4,5},{5,6},{6,7},{15,8},{8,9},{9,10... | collective-permute-start | bytes 3145736 | tf_op jit(solution)/shard_map/ppermute | solution.py:10
  170.5 16.5 %collective-permute-start.6 = (bf16[32,4,2048]{2,1,0:T(4,128)(2,1)S(1)}, bf16[32,4,2048]{2,1,0:T(4,128)(2,1)S(1)}, u32[]{:S(2)}, u32[]{:S(2)}) collective-permute-start(bf16[32,4,2048]{2,1,0:T(4,128)(2,1)S(1)} %fusion.18), channel_id=1, source_target_pairs={{1,0},{2,1},{3,2},{4,3},{5,4},{6,5},{7,6},{0,7},{9,8},{10,9},{11,1... | collective-permute-start | bytes 1572872 | tf_op jit(solution)/shard_map/ppermute | solution.py:10
  180.7 16.9 %collective-permute-start.2 = (bf16[32,8192]{1,0:T(8,128)(2,1)S(1)}, bf16[32,8192]{1,0:T(8,128)(2,1)S(1)}, u32[]{:S(2)}, u32[]{:S(2)}) collective-permute-start(bf16[32,8192]{1,0:T(8,128)(2,1)S(1)} %all_gather.7), channel_id=1, source_target_pairs={{7,0},{0,1},{1,2},{2,3},{3,4},{4,5},{5,6},{6,7},{15,8},{8,9},{9,10... | collective-permute-start | bytes 1572872 | tf_op jit(solution)/shard_map/ppermute | solution.py:10
  183.3 16.9 %collective-permute-start.3 = (bf16[32,8192]{1,0:T(8,128)(2,1)S(1)}, bf16[32,8192]{1,0:T(8,128)(2,1)S(1)}, u32[]{:S(2)}, u32[]{:S(2)}) collective-permute-start(bf16[32,8192]{1,0:T(8,128)(2,1)S(1)} %all_gather.7), channel_id=1, source_target_pairs={{1,0},{2,1},{3,2},{4,3},{5,4},{6,5},{7,6},{0,7},{9,8},{10,9},{11,1... | collective-permute-start | bytes 1572872 | tf_op jit(solution)/shard_map/ppermute | solution.py:10
  203.9 16.2 %copy-start.2 = (f32[8,4,8,256]{3,2,0,1:T(8,128)S(1)}, f32[8,4,8,256]{3,2,0,1:T(8,128)}, u32[]{:S(2)}) copy-start(f32[8,4,8,256]{3,2,0,1:T(8,128)} %copy.133) | copy-start | bytes 786436
  203.9 16.2 %copy-start.4 = (f32[8,4,2048]{2,0,1:T(8,128)S(1)}, f32[8,4,2048]{2,0,1:T(8,128)}, u32[]{:S(2)}) copy-start(f32[8,4,2048]{2,0,1:T(8,128)} %copy-done.3) | copy-start | bytes 786436
  214.9 6.4 %copy-start = (f32[8,32,256,1]{2,1,3,0:T(8,128)}, f32[8,32,256,1]{2,1,3,0:T(8,128)S(1)}, u32[]{:S(2)}) copy-start(f32[8,32,256,1]{2,1,3,0:T(8,128)S(1)} %fusion.4) | copy-start | bytes 786436
  231.6 51.1 %all-to-all-start.4 = ((f32[32,32,192]{2,0,1:T(8,128)}), f32[32,32,192]{2,0,1:T(8,128)S(1)}, u32[]{:S(2)}, u32[]{:S(2)}) async-start(f32[32,32,192]{2,0,1:T(8,128)} %copy.113), calls=%async_computation.4 | async-start | bytes 2097152 | tf_op jit(solution)/shard_map/all_to_all | solution.py:101
Sparse Core Ops, SparseCore 0:
  108.1 27.7 reduce-scatter.6
  189.9 30.2 reduce-scatter.8
where the time goes:
time: 339 us; the launch traced here: 337 us
  other arithmetic  133 us (39%)
  local copies, waits for them, and re-layouts  56.2 us (17%)
  matrix products  43 us (13%)
  starting transfers between devices  36.7 us (11%)
  waiting for transfers between devices  35.1 us (10%)
  blocking collectives  18.1 us (5%)
  between operations  14.5 us (4%)
    scatter-add x1, other arithmetic, body(): jax.ops.segment_sum(jnp.ones((device_count * capacity,), jnp.float32), fl...  42.6 us
    scatter-add x1, other arithmetic, body(): jax.ops.segment_sum(flat_values.T, flat_labels, surface_count + 1)  41.4 us
    scatter-add x2, other arithmetic, adjoint(): empty.at[:, flat_offsets]  26.9 us
    ppermute x8, waiting for transfers between devices, passed_along(): return lax.ppermute(block, axis, route)  24 us
    dot_general x2, matrix products, forward(): jnp.einsum('rkij,brkj->bri', matrix, picked, preferred_element_type=jnp.f...  21.8 us
    dot_general x2, matrix products, adjoint(): jnp.einsum('rkij,bri->brkj', matrix, vector.reshape(band_count, rb_count,...  21.2 us
    all_gather x2, blocking collectives, window(): gathered = lax.all_gather(vector, 'band', axis=1, tiled=True)  18.1 us
    unnamed x25, local copies, waits for them, and re-layouts  18 us
  transfers between devices with their start and end apart: 15, of which 9 were waited for; matrix products, arithmetic and copies ran while one was open for 55% of the time, Pallas kernels for 0%

commit v1 on v0

--- a/solution.py
+++ b/solution.py
@@ -2,6 +2,24 @@
 import jax.numpy as jnp
 from jax import lax
 from jax.sharding import PartitionSpec as P
+
+
+def collect(value, axis, dim):
+    ways, here, hop = (lax.axis_size(axis), lax.axis_index(axis), value.shape[dim])
+    shape = [n * ways if d == dim else n for d, n in enumerate(value.shape)]
+    full = lax.dynamic_update_slice_in_dim(
+        jnp.zeros(shape, value.dtype), value, here * hop, axis=dim
+    )
+    going_up = going_down = value
+    for far in range(1, ways // 2 + 1):
+        going_up = lax.ppermute(going_up, axis, [(d, (d + 1) % ways) for d in range(ways)])
+        full = lax.dynamic_update_slice_in_dim(full, going_up, (here - far) % ways * hop, axis=dim)
+        if 2 * far < ways:
+            going_down = lax.ppermute(going_down, axis, [(d, (d - 1) % ways) for d in range(ways)])
+            full = lax.dynamic_update_slice_in_dim(
+                full, going_down, (here + far) % ways * hop, axis=dim
+            )
+    return full
 
 
 def passed_along(block, axis, distance):
@@ -35,7 +53,7 @@
     reflect = 1.0 - emissive
 
     def window(vector):
-        gathered = lax.all_gather(vector, "band", axis=1, tiled=True)
+        gathered = collect(vector, "band", 1)
         lower_rows = passed_along(gathered, "patch", 1)
         upper_rows = passed_along(gathered, "patch", -1)
         joined = jnp.concatenate([lower_rows, gathered, upper_rows], axis=1)

time: 339 us -> 353 us (1.041)
  waiting for transfers between devices: 35.1 us -> 54.4 us
  blocking collectives: 18.1 us -> 0 us
  starting transfers between devices: 36.7 us -> 44.3 us
  local copies, waits for them, and re-layouts: 56.2 us -> 62.2 us
    all_gather x2 -> x0, blocking collectives: 18.1 us -> none  [window(): gathered = lax.all_gather(vector, 'band', axis=1, tiled=True)]
    ppermute x8, waiting for transfers between devices: 24 us -> 36.6 us  [passed_along(): return lax.ppermute(block, axis, route)]
    dynamic_update_slice x0 -> x6, local copies, waits for them, and re-layouts: none -> 6.88 us  [the longest x4 3.71 us: collect(): lax.dynamic_update_slice_in_dim(full, going_up, (here - far) % ways * hop...]
    ppermute x0 -> x6, starting transfers between devices: none -> 5.98 us  [the longest x4 3.95 us: collect(): lax.ppermute(going_up, axis, [(d, (d + 1) % ways) for d in range(ways)])]
    ppermute x0 -> x6, waiting for transfers between devices: none -> 5.36 us  [the longest x4 5.35 us: collect(): lax.ppermute(going_up, axis, [(d, (d + 1) % ways) for d in range(ways)])]
    all_to_all x1, waiting for transfers between devices: 4.1 us -> 0.12 us  [body(): lax.all_to_all(loss_weights, 'band', split_axis=1, concat_axis=0, tiled=T...]
    all_to_all x1, waiting for transfers between devices: 0.01 us -> 3.68 us  [body(): lax.all_to_all(blackbody, 'band', split_axis=1, concat_axis=0, tiled=True)]
    unnamed x25 -> x41, local copies, waits for them, and re-layouts: 18 us -> 18.3 us
  transfers between devices with their start and end apart: 15 -> 21, of which waited for: 9 -> 11; matrix products, arithmetic and copies ran while one was open for 55% -> 54% of each run, Pallas kernels for 0% -> 0%
where the time goes in v1:
time: 353 us; the launch traced here: 351 us
  other arithmetic  132 us (37%)
  local copies, waits for them, and re-layouts  62.2 us (18%)
  waiting for transfers between devices  54.4 us (15%)
  starting transfers between devices  44.3 us (13%)
  matrix products  43.5 us (12%)
  between operations  14.6 us (4%)
    scatter-add x1, other arithmetic, body(): jax.ops.segment_sum(jnp.ones((device_count * capacity,), jnp.float32), fl...  42.6 us
    scatter-add x1, other arithmetic, body(): jax.ops.segment_sum(flat_values.T, flat_labels, surface_count + 1)  41.4 us
    ppermute x8, waiting for transfers between devices, passed_along(): return lax.ppermute(block, axis, route)  36.6 us
    scatter-add x2, other arithmetic, adjoint(): empty.at[:, flat_offsets]  27 us
    dot_general x2, matrix products, forward(): jnp.einsum('rkij,brkj->bri', matrix, picked, preferred_element_type=jnp.f...  22.2 us
    dot_general x2, matrix products, adjoint(): jnp.einsum('rkij,bri->brkj', matrix, vector.reshape(band_count, rb_count,...  21.2 us
    unnamed x41, local copies, waits for them, and re-layouts  18.3 us
    ppermute x8, starting transfers between devices, passed_along(): return lax.ppermute(block, axis, route)  11.9 us
  transfers between devices with their start and end apart: 21, of which 11 were waited for; matrix products, arithmetic and copies ran while one was open for 54% of the time, Pallas kernels for 0%

profile of v1, /device:TPU:1, one launch (start us, length us, event | category | flops | bytes accessed | tf_op | source)
XLA Modules:
  0.0 351.2 jit_solution(5567197854694126297)
XLA Ops:
  7.2 4.4 %all-to-all-start = ((f32[8,4,2048]{2,0,1:T(8,128)}), f32[8,4,2048]{2,0,1:T(8,128)S(1)}, u32[]{:S(2)}, u32[]{:S(2)}) async-start(f32[8,4,2048]{2,0,1:T(8,128)} %bitcast.219), calls=%async_computation | async-start | bytes 524288 | tf_op jit(solution)/shard_map/all_to_all | solution.py:35
  13.2 9.1 %reduce-window.6 = s32[32,16,128]{2,1,0:T(8,128)S(1)} reduce-window(s32[32,16,128]{2,1,0:T(8,128)S(1)} %fusion.35, s32[]{:T(128)} %constant.79.clone.1), window={size=1x1x128 pad=0_0x0_0x127_0}, to_apply=%region_0.1 | reduce-window | flops 8323072 | bytes 524292 | tf_op jit(solution)/shard_map/reduce-window
  24.2 8.2 %scatter_custom_fusion.4 = s32[6144]{0:T(1024)S(1)} fusion(s32[2048]{0:T(1024)S(1)} %broadcast_select_fusion.1, s32[2048]{0:T(1024)} %bitcast.226, s32[]{:T(128)} %constant.94.clone.1), kind=kCustom, calls=%fused_computation.78 | custom fusion | bytes 25088
  33.3 3.6 %all-to-all-start.1 = ((f32[8,4,2048]{2,0,1:T(8,128)}), f32[8,4,2048]{2,0,1:T(8,128)S(1)}, u32[]{:S(2)}, u32[]{:S(2)}) async-start(f32[8,4,2048]{2,0,1:T(8,128)} %bitcast.2), calls=%async_computation.1 | async-start | bytes 524288 | tf_op jit(solution)/shard_map/all_to_all | solution.py:36
  37.5 3.7 %all-to-all-done.1 = f32[8,4,2048]{2,0,1:T(8,128)S(1)} async-done(((f32[8,4,2048]{2,0,1:T(8,128)}), f32[8,4,2048]{2,0,1:T(8,128)S(1)}, u32[]{:S(2)}, u32[]{:S(2)}) %all-to-all-start.1) | async-done | bytes 262176 | tf_op jit(solution)/shard_map/all_to_all | solution.py:36
  41.2 3.4 all-to-all-start.3
  44.6 0.9 broadcast.223.clone
  46.2 1.4 collective-permute-start
  47.6 0.9 collective-permute-start.1
  48.8 9.7 %all-to-all-start.2 = ((s32[1,32,192]{2,0,1:T(1,128)}), s32[1,32,192]{2,0,1:T(1,128)}, u32[]{:S(2)}, u32[]{:S(2)}) async-start(s32[1,32,192]{2,0,1:T(1,128)} %reshape.309), calls=%async_computation.2 | async-start | bytes 65536 | tf_op jit(solution)/shard_map/all_to_all | solution.py:120
  58.6 10.6 %fusion.2 = f32[8,32,16,256]{3,1,2,0:T(8,128)} fusion(bf16[1,1,8,16,256,256]{5,4,3,2,1,0:T(8,128)(2,1)} %param.10, bf16[32,8,256,1]{2,1,0,3:T(8,128)(2,1)S(1)} %bitcast.218), kind=kOutput, calls=%fused_computation.10 | convolution fusion | flops 536870912 | bytes 21102592 | tf_op jit(solution)/shard_map/rkij,bri->brkj/dot_general | solution.py:69
  69.6 13.6 %scatter_fusion = f32[32,96,256]{2,0,1:T(8,128)S(1)} fusion(f32[32,96,256]{2,0,1:T(8,128)S(1)} %broadcast.230.clone, s32[128]{0:T(128)} %fusion.45, f32[128,32,256]{2,1,0:T(8,128)} %bitcast.199), kind=kCustom, calls=%fused_computation.2 | custom fusion | flops 1048576 | bytes 12583424 | tf_op jit(solution)/shard_map/scatter-add | solution.py:76
  83.2 3.5 copy.80
  86.7 3.4 reshape.298
  90.3 1.7 collective-permute-start.11
  92.3 1.2 collective-permute-start.2
  94.2 1.6 constant_dynamic-update-slice_fusion.5
  95.8 1.5 collective-permute-done.2
  98.0 2.9 collective-permute-start.3
  101.0 7.6 %collective-permute-done.10 = bf16[32,4,2048]{2,1,0:T(4,128)(2,1)S(1)} collective-permute-done((bf16[32,4,2048]{2,1,0:T(4,128)(2,1)S(1)}, bf16[32,4,2048]{2,1,0:T(4,128)(2,1)S(1)}, u32[]{:S(2)}, u32[]{:S(2)}) %collective-permute-start.10) | collective-permute-done | bytes 524320 | tf_op jit(solution)/shard_map/ppermute | solution.py:28
  108.7 3.5 collective-permute-done.11
  112.6 1.6 copy.83
  114.5 6.2 %collective-permute-done.3 = bf16[32,8192]{1,0:T(8,128)(2,1)S(1)} collective-permute-done((bf16[32,8192]{1,0:T(8,128)(2,1)}, bf16[32,8192]{1,0:T(8,128)(2,1)S(1)}, u32[]{:S(2)}, u32[]{:S(2)}) %collective-permute-start.3) | collective-permute-done | bytes 524320 | tf_op jit(solution)/shard_map/ppermute | solution.py:28
  120.7 1.1 pad_maximum_fusion
  121.8 1.4 copy.141
  123.2 2.1 gather_fusion
  125.3 11.1 %fusion.10 = f32[8,4,8,256]{3,2,1,0:T(8,128)S(1)} fusion(bf16[32,8,16,256]{3,0,2,1:T(8,128)(2,1)S(1)} %bitcast.202, bf16[1,1,8,16,256,256]{5,4,3,2,1,0:T(8,128)(2,1)} %param.10), kind=kOutput, calls=%fused_computation.22 | convolution fusion | flops 536870912 | bytes 19136512 | tf_op jit(solution)/shard_map/rkij,brkj->bri/dot_general | solution.py:65
  136.5 0.9 broadcast.223
  138.1 1.3 collective-permute-start.5
  140.0 1.1 collective-permute-start.6
  141.1 3.8 %collective-permute-done.5 = bf16[32,2048]{1,0:T(8,128)(2,1)S(1)} collective-permute-done((bf16[32,2048]{1,0:T(8,128)(2,1)}, bf16[32,2048]{1,0:T(8,128)(2,1)S(1)}, u32[]{:S(2)}, u32[]{:S(2)}) %collective-permute-start.5) | collective-permute-done | bytes 131104 | tf_op jit(solution)/shard_map/ppermute | solution.py:15
  144.9 1.0 copy.115
  145.9 10.6 %fusion = f32[8,32,16,256]{3,1,2,0:T(8,128)} fusion(bf16[1,1,8,16,256,256]{5,4,3,2,1,0:T(8,128)(2,1)} %param.10, bf16[32,8,256,1]{2,1,0,3:T(8,128)(2,1)S(1)} %bitcast.217), kind=kOutput, calls=%fused_computation.8 | convolution fusion | flops 536870912 | bytes 21102592 | tf_op jit(solution)/shard_map/rkij,bri->brkj/dot_general | solution.py:69
  157.2 13.5 %scatter_fusion.1 = f32[32,96,256]{2,0,1:T(8,128)S(1)} fusion(f32[32,96,256]{2,0,1:T(8,128)S(1)} %broadcast.230, s32[128]{0:T(128)S(1)} %copy-done.12, f32[128,32,256]{2,1,0:T(8,128)} %bitcast.198), kind=kCustom, calls=%fused_computation.3 | custom fusion | flops 1048576 | bytes 12583424 | tf_op jit(solution)/shard_map/scatter-add | solution.py:76
  170.7 3.5 copy.85
  174.1 3.4 reshape.302
  177.7 3.9 %collective-permute-start.13 = (f32[32,4,2048]{2,1,0:T(4,128)S(1)}, f32[32,4,2048]{2,1,0:T(4,128)S(1)}, u32[]{:S(2)}, u32[]{:S(2)}) collective-permute-start(f32[32,4,2048]{2,1,0:T(4,128)S(1)} %get-tuple-element.19), channel_id=1, source_target_pairs={{7,0},{0,1},{1,2},{2,3},{3,4},{4,5},{5,6},{6,7},{15,8},{8,9},{9,10... | collective-permute-start | bytes 3145736 | tf_op jit(solution)/shard_map/ppermute | solution.py:28
  182.6 1.6 constant_dynamic-update-slice_fusion.1
  184.2 1.6 constant_dynamic-update-slice_fusion
  185.8 1.7 collective-permute-start.8
  187.5 1.4 collective-permute-start.9
  189.0 8.7 %collective-permute-done.12 = bf16[32,4,2048]{2,1,0:T(4,128)(2,1)S(1)} collective-permute-done((bf16[32,4,2048]{2,1,0:T(4,128)(2,1)S(1)}, bf16[32,4,2048]{2,1,0:T(4,128)(2,1)S(1)}, u32[]{:S(2)}, u32[]{:S(2)}) %collective-permute-start.12) | collective-permute-done | bytes 524320 | tf_op jit(solution)/shard_map/ppermute | solution.py:28
  197.6 3.3 collective-permute-done.13
  201.4 1.6 copy.88
  203.0 7.3 %collective-permute-done.8 = bf16[32,8192]{1,0:T(8,128)(2,1)S(1)} collective-permute-done((bf16[32,8192]{1,0:T(8,128)(2,1)}, bf16[32,8192]{1,0:T(8,128)(2,1)S(1)}, u32[]{:S(2)}, u32[]{:S(2)}) %collective-permute-start.8) | collective-permute-done | bytes 524320 | tf_op jit(solution)/shard_map/ppermute | solution.py:28
  210.3 1.1 pad_maximum_fusion.1
  211.5 1.4 copy.140
  212.8 2.1 gather_fusion.1
  215.0 11.1 %fusion.4 = f32[8,32,256,1]{2,1,3,0:T(8,128)S(1)} fusion(bf16[32,8,16,256]{3,0,2,1:T(8,128)(2,1)S(1)} %bitcast.201, bf16[1,1,8,16,256,256]{5,4,3,2,1,0:T(8,128)(2,1)} %param.10), kind=kOutput, calls=%fused_computation.12 | convolution fusion | flops 536870912 | bytes 19136512 | tf_op jit(solution)/shard_map/rkij,brkj->bri/dot_general | solution.py:65
  226.2 8.6 %reduce-scatter.9.cloned.1.call-done = f32[32,1,2048]{2,0,1:T(8,128)} async-done(((f32[32,4,2048]{2,0,1:T(8,128)}), f32[32,1,2048]{2,0,1:T(8,128)}) %reduce-scatter.9.cloned.1.call-update) | async-done | bytes 262160
  234.8 1.1 fusion.29
  235.9 1.3 copy.90
  237.2 6.7 %scatter_custom_fusion.5 = f32[32,6144]{0,1:T(8,128)S(1)} fusion(s32[2048]{0:T(1024)} %broadcast_select_fusion, f32[2048,32]{1,0:T(8,128)} %copy.90, f32[]{:T(128)} %constant.93.clone.1), kind=kCustom, calls=%fused_computation.20 | custom fusion | bytes 786944
  244.0 2.2 copy.91
  246.2 5.0 %all-to-all-start.4 = ((f32[32,32,192]{2,0,1:T(8,128)}), f32[32,32,192]{2,0,1:T(8,128)S(1)}, u32[]{:S(2)}, u32[]{:S(2)}) async-start(f32[32,32,192]{2,0,1:T(8,128)} %copy.91), calls=%async_computation.4 | async-start | bytes 2097152 | tf_op jit(solution)/shard_map/all_to_all | solution.py:119
  251.2 0.8 reduce.4
  252.1 42.6 %scatter_custom_fusion.3 = f32[1025]{0:T(1024)S(1)} fusion(s32[6144]{0:T(1024)S(1)} %reshape.348, f32[6144]{0:T(1024)S(1)} %broadcast.249, f32[]{:T(128)} %constant.93.clone.1), kind=kCustom, calls=%fused_computation.87 | custom fusion | flops 6144 | bytes 4104 | tf_op jit(solution)/shard_map/scatter-add | solution.py:127
  294.8 1.1 copy.76
  296.0 1.0 copy.94
  297.6 1.3 reshape.305
  298.9 2.0 copy.93
  300.9 41.4 %scatter_custom_fusion.2 = f32[1025,32]{1,0:T(8,128)} fusion(s32[6144]{0:T(1024)S(1)} %reshape.348, f32[6144,32]{1,0:T(8,128)S(1)} %copy.93, f32[]{:T(128)} %constant.93.clone.1), kind=kCustom, calls=%fused_computation.37 | custom fusion | flops 196608 | bytes 131204 | tf_op jit(solution)/shard_map/scatter-add | solution.py:124
  342.3 1.2 fusion.19
  343.5 0.8 copy.95
  (100 shorter events, 13.5 us)
Async XLA Ops:
  7.2 16.7 %copy-start.16 = (s32[2]{0:T(128)S(1)}, s32[2]{0:T(128)}, u32[]{:S(2)}) copy-start(s32[2]{0:T(128)} %constant.106) | copy-start | bytes 28
  7.2 16.8 %copy-start.13 = (s32[3]{0:T(128)S(1)}, s32[3]{0:T(128)}, u32[]{:S(2)}) copy-start(s32[3]{0:T(128)} %constant.100) | copy-start | bytes 40
  7.2 16.9 %copy-start.15 = (s32[3]{0:T(128)S(1)}, s32[3]{0:T(128)}, u32[]{:S(2)}) copy-start(s32[3]{0:T(128)} %constant.103) | copy-start | bytes 40
  7.2 26.0 %copy-start.14 = (s32[2]{0:T(128)S(1)}, s32[2]{0:T(128)}, u32[]{:S(2)}) copy-start(s32[2]{0:T(128)} %constant.109) | copy-start | bytes 28
  7.2 16.6 %copy-start.11 = (s32[1,1,2048,1]{2,3,1,0:T(1,128)S(1)}, s32[1,1,2048,1]{2,3,1,0:T(1,128)}, u32[]{:S(2)}) copy-start(s32[1,1,2048,1]{2,3,1,0:T(1,128)} %param.12) | copy-start | bytes 24580
  7.2 26.1 %all-to-all-start = ((f32[8,4,2048]{2,0,1:T(8,128)}), f32[8,4,2048]{2,0,1:T(8,128)S(1)}, u32[]{:S(2)}, u32[]{:S(2)}) async-start(f32[8,4,2048]{2,0,1:T(8,128)} %bitcast.219), calls=%async_computation | async-start | bytes 524288 | tf_op jit(solution)/shard_map/all_to_all | solution.py:35
  33.3 7.9 %all-to-all-start.1 = ((f32[8,4,2048]{2,0,1:T(8,128)}), f32[8,4,2048]{2,0,1:T(8,128)S(1)}, u32[]{:S(2)}, u32[]{:S(2)}) async-start(f32[8,4,2048]{2,0,1:T(8,128)} %bitcast.2), calls=%async_computation.1 | async-start | bytes 524288 | tf_op jit(solution)/shard_map/all_to_all | solution.py:36
  41.2 28.1 %copy-start = (f32[8,4,2048]{2,0,1:T(8,128)}, f32[8,4,2048]{2,0,1:T(8,128)S(1)}, u32[]{:S(2)}) copy-start(f32[8,4,2048]{2,0,1:T(8,128)S(1)} %all-to-all-done.1) | copy-start | bytes 786436
  41.2 7.6 %all-to-all-start.3 = ((f32[8,4,2048]{2,0,1:T(8,128)}), f32[8,4,2048]{2,0,1:T(8,128)S(1)}, u32[]{:S(2)}, u32[]{:S(2)}) async-start(f32[8,4,2048]{2,0,1:T(8,128)} %bitcast.30), calls=%async_computation.3 | async-start | bytes 524288 | tf_op jit(solution)/shard_map/all_to_all | solution.py:37
  46.2 46.1 %collective-permute-start = (bf16[32,2048]{1,0:T(8,128)(2,1)}, bf16[32,2048]{1,0:T(8,128)(2,1)S(1)}, u32[]{:S(2)}, u32[]{:S(2)}) collective-permute-start(bf16[32,2048]{1,0:T(8,128)(2,1)} %get-tuple-element.17), channel_id=1, source_target_pairs={{0,8},{8,16},{16,24},{24,0},{1,9},{9,17},{17,25},{25,1},{2,10},{10... | collective-permute-start | bytes 393224 | tf_op jit(solution)/shard_map/ppermute | solution.py:15
  47.6 46.6 %collective-permute-start.1 = (bf16[32,2048]{1,0:T(8,128)(2,1)}, bf16[32,2048]{1,0:T(8,128)(2,1)}, u32[]{:S(2)}, u32[]{:S(2)}) collective-permute-start(bf16[32,2048]{1,0:T(8,128)(2,1)} %get-tuple-element.17), channel_id=1, source_target_pairs={{0,24},{8,0},{16,8},{24,16},{1,25},{9,1},{17,9},{25,17},{2,26},{10... | collective-permute-start | bytes 393224 | tf_op jit(solution)/shard_map/ppermute | solution.py:18
  48.6 20.6 %copy-start.7 = (f32[4,8,8,256]{3,2,1,0:T(8,128)}, f32[4,8,8,256]{3,2,1,0:T(8,128)S(1)}, u32[]{:S(2)}) copy-start(f32[4,8,8,256]{3,2,1,0:T(8,128)S(1)} %copy.113) | copy-start | bytes 786436
  48.8 20.5 %copy-start.5 = (f32[8,4,2048]{2,0,1:T(8,128)}, f32[8,4,2048]{2,0,1:T(8,128)S(1)}, u32[]{:S(2)}) copy-start(f32[8,4,2048]{2,0,1:T(8,128)S(1)} %all-to-all-done.3) | copy-start | bytes 786436
  48.8 197.4 %all-to-all-start.2 = ((s32[1,32,192]{2,0,1:T(1,128)}), s32[1,32,192]{2,0,1:T(1,128)}, u32[]{:S(2)}, u32[]{:S(2)}) async-start(s32[1,32,192]{2,0,1:T(1,128)} %reshape.309), calls=%async_computation.2 | async-start | bytes 65536 | tf_op jit(solution)/shard_map/all_to_all | solution.py:120
  58.5 86.4 %reduce-scatter.7.cloned.1.call-start = ((), (), s32[]{:S(2)}) async-start(), calls=%async_computation.7 | async-start | bytes 1310720
  90.3 21.9 %collective-permute-start.11 = (f32[32,4,2048]{2,1,0:T(4,128)S(1)}, f32[32,4,2048]{2,1,0:T(4,128)S(1)}, u32[]{:S(2)}, u32[]{:S(2)}) collective-permute-start(f32[32,4,2048]{2,1,0:T(4,128)S(1)} %get-tuple-element.21), channel_id=1, source_target_pairs={{7,0},{0,1},{1,2},{2,3},{3,4},{4,5},{5,6},{6,7},{15,8},{8,9},{9,10... | collective-permute-start | bytes 3145736 | tf_op jit(solution)/shard_map/ppermute | solution.py:28
  92.2 16.5 %collective-permute-start.10 = (bf16[32,4,2048]{2,1,0:T(4,128)(2,1)S(1)}, bf16[32,4,2048]{2,1,0:T(4,128)(2,1)S(1)}, u32[]{:S(2)}, u32[]{:S(2)}) collective-permute-start(bf16[32,4,2048]{2,1,0:T(4,128)(2,1)S(1)} %fusion.17), channel_id=1, source_target_pairs={{1,0},{2,1},{3,2},{4,3},{5,4},{6,5},{7,6},{0,7},{9,8},{10,9},{11,1... | collective-permute-start | bytes 1572872 | tf_op jit(solution)/shard_map/ppermute | solution.py:28
  92.3 5.1 %collective-permute-start.2 = (bf16[32,2048]{1,0:T(8,128)(2,1)S(1)}, bf16[32,2048]{1,0:T(8,128)(2,1)S(1)}, u32[]{:S(2)}, u32[]{:S(2)}) collective-permute-start(bf16[32,2048]{1,0:T(8,128)(2,1)S(1)} %collective-permute-done), channel_id=1, source_target_pairs={{0,8},{8,16},{16,24},{24,0},{1,9},{9,17},{17,25},{25,1},{2,10},{10... | collective-permute-start | bytes 393224 | tf_op jit(solution)/shard_map/ppermute | solution.py:15
  98.0 22.6 %collective-permute-start.3 = (bf16[32,8192]{1,0:T(8,128)(2,1)}, bf16[32,8192]{1,0:T(8,128)(2,1)S(1)}, u32[]{:S(2)}, u32[]{:S(2)}) collective-permute-start(bf16[32,8192]{1,0:T(8,128)(2,1)} %constant_dynamic-update-slice_fusion.4), channel_id=1, source_target_pairs={{7,0},{0,1},{1,2},{2,3},{3,4},{4,5},{5,6},{6,7},{15,8},{8,9},{9,10... | collective-permute-start | bytes 1572872 | tf_op jit(solution)/shard_map/ppermute | solution.py:28
  100.9 19.8 %collective-permute-start.4 = (bf16[32,8192]{1,0:T(8,128)(2,1)}, bf16[32,8192]{1,0:T(8,128)(2,1)S(1)}, u32[]{:S(2)}, u32[]{:S(2)}) collective-permute-start(bf16[32,8192]{1,0:T(8,128)(2,1)} %constant_dynamic-update-slice_fusion.4), channel_id=1, source_target_pairs={{1,0},{2,1},{3,2},{4,3},{5,4},{6,5},{7,6},{0,7},{9,8},{10,9},{11,1... | collective-permute-start | bytes 1572872 | tf_op jit(solution)/shard_map/ppermute | solution.py:28
  114.3 120.5 %reduce-scatter.9.cloned.1.call-start = ((), (), s32[]{:S(2)}) async-start(), calls=%async_computation.8 | async-start | bytes 1310720
  125.3 12.1 %copy-start.1 = (f32[8,4,2048]{2,0,1:T(8,128)S(1)}, f32[8,4,2048]{2,0,1:T(8,128)}, u32[]{:S(2)}) copy-start(f32[8,4,2048]{2,0,1:T(8,128)} %copy-done) | copy-start | bytes 786436
  125.3 20.6 %copy-start.8 = (f32[4,8,8,256]{3,2,1,0:T(8,128)S(1)}, f32[4,8,8,256]{3,2,1,0:T(8,128)}, u32[]{:S(2)}) copy-start(f32[4,8,8,256]{3,2,1,0:T(8,128)} %copy-done.7) | copy-start | bytes 786436
  136.5 20.1 %copy-start.9 = (f32[8,4,8,256]{3,2,0,1:T(8,128)}, f32[8,4,8,256]{3,2,0,1:T(8,128)S(1)}, u32[]{:S(2)}) copy-start(f32[8,4,8,256]{3,2,0,1:T(8,128)S(1)} %copy.111) | copy-start | bytes 786436
  138.1 6.8 %collective-permute-start.5 = (bf16[32,2048]{1,0:T(8,128)(2,1)}, bf16[32,2048]{1,0:T(8,128)(2,1)S(1)}, u32[]{:S(2)}, u32[]{:S(2)}) collective-permute-start(bf16[32,2048]{1,0:T(8,128)(2,1)} %get-tuple-element.13), channel_id=1, source_target_pairs={{0,8},{8,16},{16,24},{24,0},{1,9},{9,17},{17,25},{25,1},{2,10},{10... | collective-permute-start | bytes 393224 | tf_op jit(solution)/shard_map/ppermute | solution.py:15
  140.0 42.7 %collective-permute-start.6 = (bf16[32,2048]{1,0:T(8,128)(2,1)}, bf16[32,2048]{1,0:T(8,128)(2,1)}, u32[]{:S(2)}, u32[]{:S(2)}) collective-permute-start(bf16[32,2048]{1,0:T(8,128)(2,1)} %get-tuple-element.13), channel_id=1, source_target_pairs={{0,24},{8,0},{16,8},{24,16},{1,25},{9,1},{17,9},{25,17},{2,26},{10... | collective-permute-start | bytes 393224 | tf_op jit(solution)/shard_map/ppermute | solution.py:18
  144.9 39.3 %collective-permute-start.7 = (bf16[32,2048]{1,0:T(8,128)(2,1)S(1)}, bf16[32,2048]{1,0:T(8,128)(2,1)}, u32[]{:S(2)}, u32[]{:S(2)}) collective-permute-start(bf16[32,2048]{1,0:T(8,128)(2,1)S(1)} %collective-permute-done.5), channel_id=1, source_target_pairs={{0,8},{8,16},{16,24},{24,0},{1,9},{9,17},{17,25},{25,1},{2,10},{10... | collective-permute-start | bytes 393224 | tf_op jit(solution)/shard_map/ppermute | solution.py:15
  156.6 0.6 copy-start.12
  177.7 23.2 %collective-permute-start.13 = (f32[32,4,2048]{2,1,0:T(4,128)S(1)}, f32[32,4,2048]{2,1,0:T(4,128)S(1)}, u32[]{:S(2)}, u32[]{:S(2)}) collective-permute-start(f32[32,4,2048]{2,1,0:T(4,128)S(1)} %get-tuple-element.19), channel_id=1, source_target_pairs={{7,0},{0,1},{1,2},{2,3},{3,4},{4,5},{5,6},{6,7},{15,8},{8,9},{9,10... | collective-permute-start | bytes 3145736 | tf_op jit(solution)/shard_map/ppermute | solution.py:28
  181.8 15.8 %collective-permute-start.12 = (bf16[32,4,2048]{2,1,0:T(4,128)(2,1)S(1)}, bf16[32,4,2048]{2,1,0:T(4,128)(2,1)S(1)}, u32[]{:S(2)}, u32[]{:S(2)}) collective-permute-start(bf16[32,4,2048]{2,1,0:T(4,128)(2,1)S(1)} %fusion.18), channel_id=1, source_target_pairs={{1,0},{2,1},{3,2},{4,3},{5,4},{6,5},{7,6},{0,7},{9,8},{10,9},{11,1... | collective-permute-start | bytes 1572872 | tf_op jit(solution)/shard_map/ppermute | solution.py:28
  185.8 24.5 %collective-permute-start.8 = (bf16[32,8192]{1,0:T(8,128)(2,1)}, bf16[32,8192]{1,0:T(8,128)(2,1)S(1)}, u32[]{:S(2)}, u32[]{:S(2)}) collective-permute-start(bf16[32,8192]{1,0:T(8,128)(2,1)} %constant_dynamic-update-slice_fusion), channel_id=1, source_target_pairs={{7,0},{0,1},{1,2},{2,3},{3,4},{4,5},{5,6},{6,7},{15,8},{8,9},{9,10... | collective-permute-start | bytes 1572872 | tf_op jit(solution)/shard_map/ppermute | solution.py:28
  187.5 22.8 %collective-permute-start.9 = (bf16[32,8192]{1,0:T(8,128)(2,1)}, bf16[32,8192]{1,0:T(8,128)(2,1)S(1)}, u32[]{:S(2)}, u32[]{:S(2)}) collective-permute-start(bf16[32,8192]{1,0:T(8,128)(2,1)} %constant_dynamic-update-slice_fusion), channel_id=1, source_target_pairs={{1,0},{2,1},{3,2},{4,3},{5,4},{6,5},{7,6},{0,7},{9,8},{10,9},{11,1... | collective-permute-start | bytes 1572872 | tf_op jit(solution)/shard_map/ppermute | solution.py:28
  215.0 19.8 %copy-start.2 = (f32[8,4,2048]{2,0,1:T(8,128)S(1)}, f32[8,4,2048]{2,0,1:T(8,128)}, u32[]{:S(2)}) copy-start(f32[8,4,2048]{2,0,1:T(8,128)} %copy-done) | copy-start | bytes 786436
  215.0 19.8 %copy-start.6 = (f32[8,4,2048]{2,0,1:T(8,128)S(1)}, f32[8,4,2048]{2,0,1:T(8,128)}, u32[]{:S(2)}) copy-start(f32[8,4,2048]{2,0,1:T(8,128)} %copy-done.5) | copy-start | bytes 786436
  215.0 19.8 %copy-start.10 = (f32[8,4,8,256]{3,2,0,1:T(8,128)S(1)}, f32[8,4,8,256]{3,2,0,1:T(8,128)}, u32[]{:S(2)}) copy-start(f32[8,4,8,256]{3,2,0,1:T(8,128)} %copy-done.9) | copy-start | bytes 786436
  226.1 9.8 %copy-start.4 = (f32[8,32,256,1]{2,1,3,0:T(8,128)}, f32[8,32,256,1]{2,1,3,0:T(8,128)S(1)}, u32[]{:S(2)}) copy-start(f32[8,32,256,1]{2,1,3,0:T(8,128)S(1)} %fusion.4) | copy-start | bytes 786436
  246.2 49.8 %copy-start.3 = (f32[8,4,2048]{2,0,1:T(8,128)S(1)}, f32[8,4,2048]{2,0,1:T(8,128)}, u32[]{:S(2)}) copy-start(f32[8,4,2048]{2,0,1:T(8,128)} %copy-done) | copy-start | bytes 786436
  246.2 50.8 %all-to-all-start.4 = ((f32[32,32,192]{2,0,1:T(8,128)}), f32[32,32,192]{2,0,1:T(8,128)S(1)}, u32[]{:S(2)}, u32[]{:S(2)}) async-start(f32[32,32,192]{2,0,1:T(8,128)} %copy.91), calls=%async_computation.4 | async-start | bytes 2097152 | tf_op jit(solution)/shard_map/all_to_all | solution.py:119
Sparse Core Ops, SparseCore 0:
  114.4 29.7 reduce-scatter.6
  203.1 31.6 reduce-scatter.8
